TPU v7x, 32 devices: a whole 2x2x4 slice. The times are simulated.
32 devices in a mesh: gx: 4 (over z), gy: 8 (over y, x, core).
Axes of the slice: x: 2, y: 2, z: 4, core: 2. Of those that a mesh axis runs over, the one named last changes fastest.
Arguments:
- features: bfloat16 [8192, 512], P(('gx', 'gy')), may hold values from -6 to 6
- cotangent: bfloat16 [8192, 512], P(('gx', 'gy')), may hold values from -6 to 6
- self_weight: bfloat16 [3, 512, 512], replicated, may hold values from -0.25 to 0.25
- neigh_weight: bfloat16 [3, 512, 512], replicated, may hold values from -0.25 to 0.25
- block_val: bfloat16 [64, 4, 128, 128], P(('gx', 'gy')), may hold values from -0.25 to 0.25
- block_col: int32 [64, 4], P(('gx', 'gy')), may hold values from 0 to 5
- send_idx: int32 [32, 32, 16], P(('gx', 'gy')), may hold values from 0 to 255
- send_count: int32 [32, 32], P(('gx', 'gy')), may hold values from 0 to 16, as said below
Outputs:
- self_grad: bfloat16 [3, 512, 512], replicated
- neigh_grad: bfloat16 [3, 512, 512], replicated
- input_grad: bfloat16 [8192, 512], P(('gx', 'gy'))
Inputs may be any that keep to these rules, and one draw needn't show every extreme that they name: `send_count`: at most 16 rows from one device to one peer; in every draw some receivers get exactly 16 from every device.
All inputs are finite; a program needn't handle non-finite values.
Results may differ from a plain program's by a relative error of at most 0.02.
Values may be sent and summed in bfloat16 or wider, within the bound.
No kernel may reach another device: no remote copies, remote signals or barrier semaphores. Data moves between devices by JAX's collectives and lax.ppermute only.
A program may use at most 128 MiB of HBM per device.

v0:
```python
import math
import jax
import jax.numpy as jnp
from jax import lax
from jax.sharding import PartitionSpec as P


def gather_sum(extended, values, columns, tile):
    width = extended.shape[1]
    tiled = extended.reshape(-1, tile, width)[columns]
    total = jnp.einsum("rbij,rbjd->rid", values, tiled, preferred_element_type=jnp.float32)
    return total.reshape(-1, width)


def spread_back(upstream, values, columns, ext_tiles, tile):
    width = upstream.shape[1]
    contrib = jnp.einsum(
        "rbij,rid->rbjd",
        values,
        upstream.reshape(-1, tile, width),
        preferred_element_type=jnp.float32,
    )
    onehot = (
        columns.reshape(-1)[None, :] == jnp.arange(ext_tiles, dtype=jnp.int32)[:, None]
    ).astype(jnp.float32)
    total = jnp.einsum(
        "cn,njd->cjd", onehot, contrib.reshape(-1, tile, width), precision=lax.Precision.HIGHEST
    )
    return total.reshape(-1, width)


def per_device(
    features, cotangent, self_weight, neigh_weight, block_val, block_col, send_idx, send_count
):
    outer = lax.axis_size("gx")
    inner = lax.axis_size("gy")
    devices = outer * inner
    node_rows, width = features.shape
    tile = block_val.shape[2]
    layers = self_weight.shape[0]
    slots = send_idx.shape[2]
    halo_rows = devices * slots
    ext_tiles = (node_rows + halo_rows) // tile
    scale = 1.0 / math.sqrt(node_rows * devices)
    row_ids = send_idx.reshape(-1)
    live = (jnp.arange(slots, dtype=jnp.int32)[None, :] < send_count.reshape(-1)[:, None]).reshape(
        -1, 1
    )
    hiddens = [features]
    aggregates = []
    preacts = []
    hidden = features
    for layer_at in range(layers):
        picked = jnp.where(live, jnp.take(hidden, row_ids, axis=0), jnp.zeros((), hidden.dtype))
        picked = picked.reshape(outer, inner, slots, width)
        send_arrived = lax.all_to_all(
            lax.all_to_all(picked, "gx", split_axis=0, concat_axis=0, tiled=True),
            "gy",
            split_axis=1,
            concat_axis=1,
            tiled=True,
        )
        extended = jnp.concatenate([hidden, send_arrived.reshape(halo_rows, width)], axis=0)
        aggregate = gather_sum(extended, block_val, block_col, tile).astype(jnp.bfloat16)
        preact = jnp.dot(
            hidden, self_weight[layer_at], preferred_element_type=jnp.float32
        ) + jnp.dot(aggregate, neigh_weight[layer_at], preferred_element_type=jnp.float32)
        aggregates.append(aggregate)
        preacts.append(preact)
        if layer_at < layers - 1:
            hidden = jax.nn.silu(preact).astype(jnp.bfloat16)
            hiddens.append(hidden)
    transposed = (((0,), (0,)), ((), ()))
    against = (((1,), (1,)), ((), ()))
    self_list = [None] * layers
    neigh_list = [None] * layers
    grad = cotangent
    for layer_at in reversed(range(layers)):
        preact = preacts[layer_at]
        sigma = jax.nn.sigmoid(preact)
        delta = (grad.astype(jnp.float32) * sigma * (1.0 + preact * (1.0 - sigma))).astype(
            jnp.bfloat16
        )
        self_term = lax.dot_general(
            hiddens[layer_at], delta, transposed, preferred_element_type=jnp.float32
        )
        neigh_term = lax.dot_general(
            aggregates[layer_at], delta, transposed, preferred_element_type=jnp.float32
        )
        self_sum, neigh_sum = lax.psum((self_term, neigh_term), ("gx", "gy"))
        self_list[layer_at] = (self_sum * scale).astype(jnp.bfloat16)
        neigh_list[layer_at] = (neigh_sum * scale).astype(jnp.bfloat16)
        own_part = lax.dot_general(
            delta, self_weight[layer_at], against, preferred_element_type=jnp.float32
        )
        upstream = lax.dot_general(
            delta, neigh_weight[layer_at], against, preferred_element_type=jnp.float32
        ).astype(jnp.bfloat16)
        ext_grad = spread_back(upstream, block_val, block_col, ext_tiles, tile)
        outgoing = ext_grad[node_rows:].astype(jnp.bfloat16).reshape(outer, inner, slots, width)
        arrived = lax.all_to_all(
            lax.all_to_all(outgoing, "gx", split_axis=0, concat_axis=0, tiled=True),
            "gy",
            split_axis=1,
            concat_axis=1,
            tiled=True,
        )
        masked = jnp.where(
            live, arrived.reshape(halo_rows, width).astype(jnp.float32), jnp.zeros((), jnp.float32)
        )
        returned = jnp.zeros((node_rows, width), jnp.float32).at[row_ids].add(masked)
        grad = (own_part + ext_grad[:node_rows] + returned).astype(jnp.bfloat16)
    self_grad = jnp.stack(self_list)
    neigh_grad = jnp.stack(neigh_list)
    return (self_grad, neigh_grad, grad)


def solution(mesh):
    return jax.shard_map(
        per_device,
        mesh=mesh,
        in_specs=(
            P(("gx", "gy"), None),
            P(("gx", "gy"), None),
            P(),
            P(),
            P(("gx", "gy"), None, None, None),
            P(("gx", "gy"), None),
            P(("gx", "gy"), None, None),
            P(("gx", "gy"), None),
        ),
        out_specs=(P(), P(), P(("gx", "gy"), None)),
        check_vma=False,
    )
```

profile of v0, /device:TPU:0, one launch (start us, length us, event | category | flops | bytes accessed | tf_op | source)
XLA Modules:
  0.0 399.9 jit_solution(2928996028955188981)
XLA Ops:
  8.9 3.0 gather_fusion.3
  12.1 20.8 %all_to_all.60 = bf16[4,8,16,512]{3,2,1,0:T(8,128)(2,1)S(1)} all-to-all(bf16[4,8,16,512]{3,2,1,0:T(8,128)(2,1)S(1)} %bitcast.184), channel_id=1, replica_groups=mesh['gx'=4,'gy'=8] {'gx'}, dimensions={0} | all-to-all | bytes 1048576 | tf_op jit(solution)/shard_map/all_to_all | solution.py:57
  33.7 3.7 all-to-all-start.1
  37.6 1.1 fusion.22
  38.7 8.5 %all-to-all-done.1 = bf16[4,8,16,512]{3,2,0,1:T(8,128)(2,1)S(1)} async-done(((bf16[4,8,16,512]{3,2,0,1:T(8,128)(2,1)}), bf16[4,8,16,512]{3,2,0,1:T(8,128)(2,1)S(1)}, u32[]{:S(2)}, u32[]{:S(2)}) %all-to-all-start.1) | async-done | bytes 524320 | tf_op jit(solution)/shard_map/all_to_all | solution.py:56
  47.3 1.6 gather_fusion
  48.9 1.6 fusion
  50.5 2.3 multiply_convert_fusion.10
  52.8 2.0 gather_fusion.4
  54.9 14.9 %all_to_all.61 = bf16[4,8,16,512]{3,2,1,0:T(8,128)(2,1)S(1)} all-to-all(bf16[4,8,16,512]{3,2,1,0:T(8,128)(2,1)S(1)} %bitcast.185), channel_id=1, replica_groups=mesh['gx'=4,'gy'=8] {'gx'}, dimensions={0} | all-to-all | bytes 1048576 | tf_op jit(solution)/shard_map/all_to_all | solution.py:57
  70.7 4.3 %all-to-all-start.3 = ((bf16[4,8,16,512]{3,2,0,1:T(8,128)(2,1)}), bf16[4,8,16,512]{3,2,0,1:T(8,128)(2,1)S(1)}, u32[]{:S(2)}, u32[]{:S(2)}) async-start(bf16[4,8,16,512]{3,2,0,1:T(8,128)(2,1)} %copy.111), calls=%async_computation.3 | async-start | bytes 1048576 | tf_op jit(solution)/shard_map/all_to_all | solution.py:56
  75.0 1.1 fusion.17
  76.1 8.6 %all-to-all-done.3 = bf16[4,8,16,512]{3,2,0,1:T(8,128)(2,1)S(1)} async-done(((bf16[4,8,16,512]{3,2,0,1:T(8,128)(2,1)}), bf16[4,8,16,512]{3,2,0,1:T(8,128)(2,1)S(1)}, u32[]{:S(2)}, u32[]{:S(2)}) %all-to-all-start.3) | async-done | bytes 524320 | tf_op jit(solution)/shard_map/all_to_all | solution.py:56
  84.8 1.6 gather_fusion.1
  86.4 1.6 fusion.1
  88.0 2.2 multiply_convert_fusion.9
  90.3 2.0 gather_fusion.5
  92.4 14.9 %all_to_all.62 = bf16[4,8,16,512]{3,2,1,0:T(8,128)(2,1)S(1)} all-to-all(bf16[4,8,16,512]{3,2,1,0:T(8,128)(2,1)S(1)} %bitcast.183), channel_id=1, replica_groups=mesh['gx'=4,'gy'=8] {'gx'}, dimensions={0} | all-to-all | bytes 1048576 | tf_op jit(solution)/shard_map/all_to_all | solution.py:57
  108.2 4.3 %all-to-all-start.5 = ((bf16[4,8,16,512]{3,2,0,1:T(8,128)(2,1)}), bf16[4,8,16,512]{3,2,0,1:T(8,128)(2,1)S(1)}, u32[]{:S(2)}, u32[]{:S(2)}) async-start(bf16[4,8,16,512]{3,2,0,1:T(8,128)(2,1)} %copy.113), calls=%async_computation.5 | async-start | bytes 1048576 | tf_op jit(solution)/shard_map/all_to_all | solution.py:56
  112.6 1.1 fusion.12
  113.7 8.5 %all-to-all-done.5 = bf16[4,8,16,512]{3,2,0,1:T(8,128)(2,1)S(1)} async-done(((bf16[4,8,16,512]{3,2,0,1:T(8,128)(2,1)}), bf16[4,8,16,512]{3,2,0,1:T(8,128)(2,1)S(1)}, u32[]{:S(2)}, u32[]{:S(2)}) %all-to-all-start.5) | async-done | bytes 524320 | tf_op jit(solution)/shard_map/all_to_all | solution.py:56
  124.0 1.5 multiply_convert_fusion.8
  125.6 1.5 convolution_convert_fusion.2
  127.5 2.1 copy.116
  129.6 2.7 fusion.43
  132.6 0.9 copy.119
  133.5 4.1 %all-to-all-start.6 = ((bf16[4,8,16,512]{3,2,1,0:T(8,128)(2,1)}), bf16[4,8,16,512]{3,2,1,0:T(8,128)(2,1)}, u32[]{:S(2)}, u32[]{:S(2)}) async-start(bf16[4,8,16,512]{3,2,1,0:T(8,128)(2,1)} %copy.119), calls=%async_computation.6 | async-start | bytes 1048576 | tf_op jit(solution)/shard_map/all_to_all | solution.py:102
  137.7 12.5 %all-to-all-done.6 = bf16[4,8,16,512]{3,2,1,0:T(8,128)(2,1)} async-done(((bf16[4,8,16,512]{3,2,1,0:T(8,128)(2,1)}), bf16[4,8,16,512]{3,2,1,0:T(8,128)(2,1)}, u32[]{:S(2)}, u32[]{:S(2)}) %all-to-all-start.6) | async-done | bytes 524320 | tf_op jit(solution)/shard_map/all_to_all | solution.py:102
  150.2 1.9 copy.120
  152.1 4.3 %all-to-all-start.7 = ((bf16[4,8,16,512]{3,2,0,1:T(8,128)(2,1)}), bf16[4,8,16,512]{3,2,0,1:T(8,128)(2,1)}, u32[]{:S(2)}, u32[]{:S(2)}) async-start(bf16[4,8,16,512]{3,2,0,1:T(8,128)(2,1)} %copy.120), calls=%async_computation.7 | async-start | bytes 1048576 | tf_op jit(solution)/shard_map/all_to_all | solution.py:101
  156.7 1.4 convolution_add_fusion.2
  158.1 8.1 %all-to-all-done.7 = bf16[4,8,16,512]{3,2,0,1:T(8,128)(2,1)} async-done(((bf16[4,8,16,512]{3,2,0,1:T(8,128)(2,1)}), bf16[4,8,16,512]{3,2,0,1:T(8,128)(2,1)}, u32[]{:S(2)}, u32[]{:S(2)}) %all-to-all-start.7) | async-done | bytes 524320 | tf_op jit(solution)/shard_map/all_to_all | solution.py:101
  166.2 1.2 copy.121
  167.5 4.0 scatter_fusion
  171.8 1.4 convolution_convert_fusion.1
  173.6 2.1 copy.123
  175.7 2.7 fusion.41
  178.7 0.9 copy.125
  179.6 4.1 %all-to-all-start.8 = ((bf16[4,8,16,512]{3,2,1,0:T(8,128)(2,1)}), bf16[4,8,16,512]{3,2,1,0:T(8,128)(2,1)}, u32[]{:S(2)}, u32[]{:S(2)}) async-start(bf16[4,8,16,512]{3,2,1,0:T(8,128)(2,1)} %copy.125), calls=%async_computation.8 | async-start | bytes 1048576 | tf_op jit(solution)/shard_map/all_to_all | solution.py:102
  183.7 2.4 fusion.54
  186.1 1.3 fusion.51
  187.8 1.3 fusion.53
  189.1 7.2 %all-to-all-done.8 = bf16[4,8,16,512]{3,2,1,0:T(8,128)(2,1)} async-done(((bf16[4,8,16,512]{3,2,1,0:T(8,128)(2,1)}), bf16[4,8,16,512]{3,2,1,0:T(8,128)(2,1)}, u32[]{:S(2)}, u32[]{:S(2)}) %all-to-all-start.8) | async-done | bytes 524320 | tf_op jit(solution)/shard_map/all_to_all | solution.py:102
  196.3 1.9 copy.126
  198.2 4.3 %all-to-all-start.9 = ((bf16[4,8,16,512]{3,2,0,1:T(8,128)(2,1)}), bf16[4,8,16,512]{3,2,0,1:T(8,128)(2,1)S(1)}, u32[]{:S(2)}, u32[]{:S(2)}) async-start(bf16[4,8,16,512]{3,2,0,1:T(8,128)(2,1)} %copy.126), calls=%async_computation.9 | async-start | bytes 1048576 | tf_op jit(solution)/shard_map/all_to_all | solution.py:101
  202.5 1.3 fusion.50
  203.9 1.4 convolution_add_fusion.1
  205.2 7.0 %all-to-all-done.9 = bf16[4,8,16,512]{3,2,0,1:T(8,128)(2,1)S(1)} async-done(((bf16[4,8,16,512]{3,2,0,1:T(8,128)(2,1)}), bf16[4,8,16,512]{3,2,0,1:T(8,128)(2,1)S(1)}, u32[]{:S(2)}, u32[]{:S(2)}) %all-to-all-start.9) | async-done | bytes 524320 | tf_op jit(solution)/shard_map/all_to_all | solution.py:101
  212.5 4.0 %scatter_fusion.1 = f32[256,512]{1,0:T(8,128)S(1)} fusion(f32[256,512]{1,0:T(8,128)S(1)} %convolution_add_fusion.1, s32[512]{0:T(512)S(1)} %bitcast.199, f32[512,512]{1,0:T(8,128)S(1)} %bitcast_select_fusion.1), kind=kCustom, calls=%fused_computation.7 | custom fusion | flops 262144 | bytes 3147776 | tf_op jit(solution)/shard_map/scatter-add | solution.py:111
  216.8 1.4 fusion.52
  218.1 1.3 convolution_bitcast_fusion
  219.5 1.4 convolution_convert_fusion
  221.3 2.1 copy.134
  223.4 2.7 fusion.39
  226.5 22.2 %all_to_all.63 = bf16[4,8,16,512]{3,2,1,0:T(8,128)(2,1)S(1)} all-to-all(bf16[4,8,16,512]{3,2,1,0:T(8,128)(2,1)S(1)} %copy.136), channel_id=1, replica_groups=mesh['gx'=4,'gy'=8] {'gx'}, dimensions={0} | all-to-all | bytes 1048576 | tf_op jit(solution)/shard_map/all_to_all | solution.py:102
  249.5 3.5 all-to-all-start.11
  253.4 1.4 convolution_add_fusion
  254.8 7.9 %all-to-all-done.11 = bf16[4,8,16,512]{3,2,0,1:T(8,128)(2,1)S(1)} async-done(((bf16[4,8,16,512]{3,2,0,1:T(8,128)(2,1)}), bf16[4,8,16,512]{3,2,0,1:T(8,128)(2,1)S(1)}, u32[]{:S(2)}, u32[]{:S(2)}) %all-to-all-start.11) | async-done | bytes 524320 | tf_op jit(solution)/shard_map/all_to_all | solution.py:101
  263.0 3.8 scatter_fusion.2
  267.5 117.8 %all-reduce.3.cloned.1.call-done = (f32[512,512]{0,1:T(8,128)}, f32[512,512]{0,1:T(8,128)}, f32[512,512]{0,1:T(8,128)}, f32[512,512]{0,1:T(8,128)}, f32[512,512]{0,1:T(8,128)}, /*index=5*/f32[512,512]{0,1:T(8,128)}) async-done(((f32[512,512]{0,1:T(8,128)}, f32[512,512]{0,1:T(8,128)}, f32[512,512]{0,1:T(8,128)}, f32[512,512]{0,1:T(8,128)}, f32[512,512]{0,1:T(8,128)}, /*index=5*/f32[512,512]{0,1:T(8,128)}), ...) | async-done | bytes 6291472 | tf_op jit(solution)/shard_map/psum | solution.py:90
  385.3 2.0 fusion.7
  387.9 1.6 copy.140
  389.5 1.8 fusion.3
  391.5 1.6 copy.139
  (92 shorter events, 14.0 us)
Async XLA Ops:
  7.2 41.7 %copy-start = (bf16[2,4,128,128]{3,2,1,0:T(8,128)(2,1)S(1)}, bf16[2,4,128,128]{3,2,1,0:T(8,128)(2,1)}, u32[]{:S(2)}) copy-start(bf16[2,4,128,128]{3,2,1,0:T(8,128)(2,1)} %param.14) | copy-start | bytes 786436
  12.1 25.4 %copy-start.17 = (s32[2,4]{1,0:T(2,128)S(1)}, s32[2,4]{1,0:T(2,128)}, u32[]{:S(2)}) copy-start(s32[2,4]{1,0:T(2,128)} %param.15) | copy-start | bytes 100
  12.1 25.5 %copy-start.1 = (bf16[256,512]{1,0:T(8,128)(2,1)S(1)}, bf16[256,512]{1,0:T(8,128)(2,1)}, u32[]{:S(2)}) copy-start(bf16[256,512]{1,0:T(8,128)(2,1)} %param.10) | copy-start | bytes 786436
  12.1 25.4 %copy-start.2 = (bf16[3,512,512]{2,1,0:T(8,128)(2,1)S(1)}, bf16[3,512,512]{2,1,0:T(8,128)(2,1)}, u32[]{:S(2)}) copy-start(bf16[3,512,512]{2,1,0:T(8,128)(2,1)} %param.12) | copy-start | bytes 4718596
  33.7 13.4 %all-to-all-start.1 = ((bf16[4,8,16,512]{3,2,0,1:T(8,128)(2,1)}), bf16[4,8,16,512]{3,2,0,1:T(8,128)(2,1)S(1)}, u32[]{:S(2)}, u32[]{:S(2)}) async-start(bf16[4,8,16,512]{3,2,0,1:T(8,128)(2,1)} %copy.109), calls=%async_computation.1 | async-start | bytes 1048576 | tf_op jit(solution)/shard_map/all_to_all | solution.py:56
  48.9 1.6 copy-start.14
  50.5 2.3 copy-start.7
  70.7 14.0 %all-to-all-start.3 = ((bf16[4,8,16,512]{3,2,0,1:T(8,128)(2,1)}), bf16[4,8,16,512]{3,2,0,1:T(8,128)(2,1)S(1)}, u32[]{:S(2)}, u32[]{:S(2)}) async-start(bf16[4,8,16,512]{3,2,0,1:T(8,128)(2,1)} %copy.111), calls=%async_computation.3 | async-start | bytes 1048576 | tf_op jit(solution)/shard_map/all_to_all | solution.py:56
  86.4 1.6 copy-start.15
  88.0 2.3 copy-start.9
  108.2 14.0 %all-to-all-start.5 = ((bf16[4,8,16,512]{3,2,0,1:T(8,128)(2,1)}), bf16[4,8,16,512]{3,2,0,1:T(8,128)(2,1)S(1)}, u32[]{:S(2)}, u32[]{:S(2)}) async-start(bf16[4,8,16,512]{3,2,0,1:T(8,128)(2,1)} %copy.113), calls=%async_computation.5 | async-start | bytes 1048576 | tf_op jit(solution)/shard_map/all_to_all | solution.py:56
  122.9 1.0 copy-start.16
  122.9 1.1 copy-start.18
  123.3 2.3 copy-start.11
  125.6 31.2 %copy-start.3 = (bf16[256,512]{1,0:T(8,128)(2,1)}, bf16[256,512]{1,0:T(8,128)(2,1)S(1)}, u32[]{:S(2)}) copy-start(bf16[256,512]{1,0:T(8,128)(2,1)S(1)} %multiply_convert_fusion.8) | copy-start | bytes 786436
  133.5 16.7 %all-to-all-start.6 = ((bf16[4,8,16,512]{3,2,1,0:T(8,128)(2,1)}), bf16[4,8,16,512]{3,2,1,0:T(8,128)(2,1)}, u32[]{:S(2)}, u32[]{:S(2)}) async-start(bf16[4,8,16,512]{3,2,1,0:T(8,128)(2,1)} %copy.119), calls=%async_computation.6 | async-start | bytes 1048576 | tf_op jit(solution)/shard_map/all_to_all | solution.py:102
  152.1 14.1 %all-to-all-start.7 = ((bf16[4,8,16,512]{3,2,0,1:T(8,128)(2,1)}), bf16[4,8,16,512]{3,2,0,1:T(8,128)(2,1)}, u32[]{:S(2)}, u32[]{:S(2)}) async-start(bf16[4,8,16,512]{3,2,0,1:T(8,128)(2,1)} %copy.120), calls=%async_computation.7 | async-start | bytes 1048576 | tf_op jit(solution)/shard_map/all_to_all | solution.py:101
  167.5 4.0 %copy-start.13 = (f32[256,512]{1,0:T(8,128)S(1)}, f32[256,512]{1,0:T(8,128)}, u32[]{:S(2)}) copy-start(f32[256,512]{1,0:T(8,128)} %get-tuple-element.28) | copy-start | bytes 1572868
  179.6 16.7 %all-to-all-start.8 = ((bf16[4,8,16,512]{3,2,1,0:T(8,128)(2,1)}), bf16[4,8,16,512]{3,2,1,0:T(8,128)(2,1)}, u32[]{:S(2)}, u32[]{:S(2)}) async-start(bf16[4,8,16,512]{3,2,1,0:T(8,128)(2,1)} %copy.125), calls=%async_computation.8 | async-start | bytes 1048576 | tf_op jit(solution)/shard_map/all_to_all | solution.py:102
  183.7 2.4 copy-start.4
  186.1 1.7 copy-start.10
  198.2 14.0 %all-to-all-start.9 = ((bf16[4,8,16,512]{3,2,0,1:T(8,128)(2,1)}), bf16[4,8,16,512]{3,2,0,1:T(8,128)(2,1)S(1)}, u32[]{:S(2)}, u32[]{:S(2)}) async-start(bf16[4,8,16,512]{3,2,0,1:T(8,128)(2,1)} %copy.126), calls=%async_computation.9 | async-start | bytes 1048576 | tf_op jit(solution)/shard_map/all_to_all | solution.py:101
  202.5 182.8 %all-reduce.3.cloned.1.call-start = ((), (), s32[]{:S(2)}) async-start(), calls=%async_computation.12 | async-start | bytes 12582912 | tf_op jit(solution)/shard_map/psum | solution.py:90
  212.5 4.1 %copy-start.12 = (f32[256,512]{1,0:T(8,128)S(1)}, f32[256,512]{1,0:T(8,128)}, u32[]{:S(2)}) copy-start(f32[256,512]{1,0:T(8,128)} %get-tuple-element.26) | copy-start | bytes 1572868
  212.5 4.3 %copy-start.8 = (bf16[2,512,128]{1,2,0:T(8,128)(2,1)S(1)}, bf16[2,512,128]{1,2,0:T(8,128)(2,1)}, u32[]{:S(2)}) copy-start(bf16[2,512,128]{1,2,0:T(8,128)(2,1)} %copy-done.7) | copy-start | bytes 786436
  249.5 13.1 %all-to-all-start.11 = ((bf16[4,8,16,512]{3,2,0,1:T(8,128)(2,1)}), bf16[4,8,16,512]{3,2,0,1:T(8,128)(2,1)S(1)}, u32[]{:S(2)}, u32[]{:S(2)}) async-start(bf16[4,8,16,512]{3,2,0,1:T(8,128)(2,1)} %copy.137), calls=%async_computation.11 | async-start | bytes 1048576 | tf_op jit(solution)/shard_map/all_to_all | solution.py:101
  385.3 2.0 copy-start.5
  385.3 2.2 copy-start.6
Sparse Core Ops, SparseCore 0:
  219.6 165.6 all-reduce.2
where the time goes:
time: 402 us; the launch traced here: 400 us
  waiting for transfers between devices  186 us (46%)
  blocking collectives  72.8 us (18%)
  matrix products  39.5 us (10%)
  local copies, waits for them, and re-layouts  34.6 us (9%)
  starting transfers between devices  32.8 us (8%)
  other arithmetic  19.4 us (5%)
  between operations  14.7 us (4%)
    psum x1, waiting for transfers between devices, per_device(): self_sum, neigh_sum = lax.psum((self_term, neigh_term), ('gx', 'gy'))  118 us
    all_to_all x3, blocking collectives, per_device(): lax.all_to_all(picked, 'gx', split_axis=0, concat_axis=0, tiled=True)  50.6 us
    all_to_all x3, waiting for transfers between devices, per_device(): lax.all_to_all(lax.all_to_all(picked, 'gx', split_axis=0, concat_axis=0,...  25.7 us
    all_to_all x3, waiting for transfers between devices, per_device(): lax.all_to_all(lax.all_to_all(outgoing, 'gx', split_axis=0, concat_axis=0...  23 us
    all_to_all x1, blocking collectives, per_device(): lax.all_to_all(outgoing, 'gx', split_axis=0, concat_axis=0, tiled=True)  22.2 us
    all_to_all x2, waiting for transfers between devices, per_device(): lax.all_to_all(outgoing, 'gx', split_axis=0, concat_axis=0, tiled=True)  19.7 us
    all_to_all x3, starting transfers between devices, per_device(): lax.all_to_all(lax.all_to_all(picked, 'gx', split_axis=0, concat_axis=0,...  12.4 us
    all_to_all x3, starting transfers between devices, per_device(): lax.all_to_all(lax.all_to_all(outgoing, 'gx', split_axis=0, concat_axis=0...  12.1 us
  transfers between devices with their start and end apart: 9, of which 9 were waited for; matrix products, arithmetic and copies ran while one was open for 7% of the time, Pallas kernels for 0%

commit v1 on v0

--- a/solution.py
+++ b/solution.py
@@ -3,6 +3,10 @@
 import jax.numpy as jnp
 from jax import lax
 from jax.sharding import PartitionSpec as P
+
+
+def _solve_trails(vec):
+    return lax.psum(lax.psum(vec, "gy"), "gx")
 
 
 def gather_sum(extended, values, columns, tile):
@@ -87,7 +91,7 @@
         neigh_term = lax.dot_general(
             aggregates[layer_at], delta, transposed, preferred_element_type=jnp.float32
         )
-        self_sum, neigh_sum = lax.psum((self_term, neigh_term), ("gx", "gy"))
+        self_sum, neigh_sum = _solve_trails((self_term, neigh_term))
         self_list[layer_at] = (self_sum * scale).astype(jnp.bfloat16)
         neigh_list[layer_at] = (neigh_sum * scale).astype(jnp.bfloat16)
         own_part = lax.dot_general(

time: 402 us -> 574 us (1.43)
  waiting for transfers between devices: 186 us -> 346 us
  blocking collectives: 72.8 us -> 85.4 us
    psum x1 -> x2, waiting for transfers between devices: 118 us -> 277 us  [_solve_trails(): return lax.psum(lax.psum(vec, 'gy'), 'gx')]
    all_to_all x1, blocking collectives: 22.2 us -> 34.8 us  [per_device(): lax.all_to_all(outgoing, 'gx', split_axis=0, concat_axis=0, tiled=True)]
  transfers between devices with their start and end apart: 9 -> 10, of which waited for: 9 -> 10; matrix products, arithmetic and copies ran while one was open for 7% -> 5% of each run, Pallas kernels for 0% -> 0%
where the time goes in v1:
time: 574 us; the launch traced here: 572 us
  waiting for transfers between devices  346 us (60%)
  blocking collectives  85.4 us (15%)
  matrix products  39.5 us (7%)
  local copies, waits for them, and re-layouts  34.6 us (6%)
  starting transfers between devices  33.2 us (6%)
  other arithmetic  18.8 us (3%)
  between operations  14.7 us (3%)
    psum x2, waiting for transfers between devices, _solve_trails(): return lax.psum(lax.psum(vec, 'gy'), 'gx')  277 us
    all_to_all x3, blocking collectives, per_device(): lax.all_to_all(picked, 'gx', split_axis=0, concat_axis=0, tiled=True)  50.6 us
    all_to_all x1, blocking collectives, per_device(): lax.all_to_all(outgoing, 'gx', split_axis=0, concat_axis=0, tiled=True)  34.8 us
    all_to_all x3, waiting for transfers between devices, per_device(): lax.all_to_all(lax.all_to_all(picked, 'gx', split_axis=0, concat_axis=0,...  25.7 us
    all_to_all x3, waiting for transfers between devices, per_device(): lax.all_to_all(lax.all_to_all(outgoing, 'gx', split_axis=0, concat_axis=0...  23 us
    all_to_all x2, waiting for transfers between devices, per_device(): lax.all_to_all(outgoing, 'gx', split_axis=0, concat_axis=0, tiled=True)  19.7 us
    all_to_all x3, starting transfers between devices, per_device(): lax.all_to_all(lax.all_to_all(picked, 'gx', split_axis=0, concat_axis=0,...  12.4 us
    all_to_all x3, starting transfers between devices, per_device(): lax.all_to_all(lax.all_to_all(outgoing, 'gx', split_axis=0, concat_axis=0...  12.3 us
  transfers between devices with their start and end apart: 10, of which 10 were waited for; matrix products, arithmetic and copies ran while one was open for 5% of the time, Pallas kernels for 0%

profile of v1, /device:TPU:0, one launch (start us, length us, event | category | flops | bytes accessed | tf_op | source)
XLA Modules:
  0.0 572.1 jit_solution(8444008624706183343)
XLA Ops:
  8.9 3.0 gather_fusion.3
  12.1 20.8 %all_to_all.60 = bf16[4,8,16,512]{3,2,1,0:T(8,128)(2,1)S(1)} all-to-all(bf16[4,8,16,512]{3,2,1,0:T(8,128)(2,1)S(1)} %bitcast.184), channel_id=1, replica_groups=mesh['gx'=4,'gy'=8] {'gx'}, dimensions={0} | all-to-all | bytes 1048576 | tf_op jit(solution)/shard_map/all_to_all | solution.py:61
  33.8 3.7 all-to-all-start.1
  37.6 1.1 fusion.22
  38.7 8.5 %all-to-all-done.1 = bf16[4,8,16,512]{3,2,0,1:T(8,128)(2,1)S(1)} async-done(((bf16[4,8,16,512]{3,2,0,1:T(8,128)(2,1)}), bf16[4,8,16,512]{3,2,0,1:T(8,128)(2,1)S(1)}, u32[]{:S(2)}, u32[]{:S(2)}) %all-to-all-start.1) | async-done | bytes 524320 | tf_op jit(solution)/shard_map/all_to_all | solution.py:60
  47.3 1.6 gather_fusion
  48.9 1.6 fusion
  50.5 2.3 multiply_convert_fusion.10
  52.8 2.0 gather_fusion.4
  54.9 14.9 %all_to_all.61 = bf16[4,8,16,512]{3,2,1,0:T(8,128)(2,1)S(1)} all-to-all(bf16[4,8,16,512]{3,2,1,0:T(8,128)(2,1)S(1)} %bitcast.185), channel_id=1, replica_groups=mesh['gx'=4,'gy'=8] {'gx'}, dimensions={0} | all-to-all | bytes 1048576 | tf_op jit(solution)/shard_map/all_to_all | solution.py:61
  70.7 4.3 all-to-all-start.3
  75.0 1.1 fusion.17
  76.1 8.6 %all-to-all-done.3 = bf16[4,8,16,512]{3,2,0,1:T(8,128)(2,1)S(1)} async-done(((bf16[4,8,16,512]{3,2,0,1:T(8,128)(2,1)}), bf16[4,8,16,512]{3,2,0,1:T(8,128)(2,1)S(1)}, u32[]{:S(2)}, u32[]{:S(2)}) %all-to-all-start.3) | async-done | bytes 524320 | tf_op jit(solution)/shard_map/all_to_all | solution.py:60
  84.8 1.6 gather_fusion.1
  86.4 1.6 fusion.1
  88.0 2.2 multiply_convert_fusion.9
  90.3 2.0 gather_fusion.5
  92.4 14.9 %all_to_all.62 = bf16[4,8,16,512]{3,2,1,0:T(8,128)(2,1)S(1)} all-to-all(bf16[4,8,16,512]{3,2,1,0:T(8,128)(2,1)S(1)} %bitcast.183), channel_id=1, replica_groups=mesh['gx'=4,'gy'=8] {'gx'}, dimensions={0} | all-to-all | bytes 1048576 | tf_op jit(solution)/shard_map/all_to_all | solution.py:61
  108.2 4.3 all-to-all-start.5
  112.6 1.1 fusion.12
  113.7 8.5 %all-to-all-done.5 = bf16[4,8,16,512]{3,2,0,1:T(8,128)(2,1)S(1)} async-done(((bf16[4,8,16,512]{3,2,0,1:T(8,128)(2,1)}), bf16[4,8,16,512]{3,2,0,1:T(8,128)(2,1)S(1)}, u32[]{:S(2)}, u32[]{:S(2)}) %all-to-all-start.5) | async-done | bytes 524320 | tf_op jit(solution)/shard_map/all_to_all | solution.py:60
  124.1 1.5 multiply_convert_fusion.8
  125.6 1.5 convolution_convert_fusion.2
  127.5 2.1 copy.116
  129.6 2.7 fusion.43
  132.6 0.9 copy.119
  133.5 4.1 all-to-all-start.6
  137.7 12.5 %all-to-all-done.6 = bf16[4,8,16,512]{3,2,1,0:T(8,128)(2,1)} async-done(((bf16[4,8,16,512]{3,2,1,0:T(8,128)(2,1)}), bf16[4,8,16,512]{3,2,1,0:T(8,128)(2,1)}, u32[]{:S(2)}, u32[]{:S(2)}) %all-to-all-start.6) | async-done | bytes 524320 | tf_op jit(solution)/shard_map/all_to_all | solution.py:106
  150.2 1.9 copy.120
  152.1 4.3 all-to-all-start.7
  156.7 1.4 convolution_add_fusion.2
  158.1 8.1 %all-to-all-done.7 = bf16[4,8,16,512]{3,2,0,1:T(8,128)(2,1)} async-done(((bf16[4,8,16,512]{3,2,0,1:T(8,128)(2,1)}), bf16[4,8,16,512]{3,2,0,1:T(8,128)(2,1)}, u32[]{:S(2)}, u32[]{:S(2)}) %all-to-all-start.7) | async-done | bytes 524320 | tf_op jit(solution)/shard_map/all_to_all | solution.py:105
  166.2 1.2 copy.121
  167.5 4.0 scatter_fusion
  171.8 1.4 convolution_convert_fusion.1
  173.6 2.1 copy.123
  175.7 2.7 fusion.41
  179.5 4.1 all-to-all-start.8
  183.7 2.4 fusion.54
  186.1 1.3 fusion.51
  187.8 1.3 fusion.53
  189.1 7.2 %all-to-all-done.8 = bf16[4,8,16,512]{3,2,1,0:T(8,128)(2,1)} async-done(((bf16[4,8,16,512]{3,2,1,0:T(8,128)(2,1)}), bf16[4,8,16,512]{3,2,1,0:T(8,128)(2,1)}, u32[]{:S(2)}, u32[]{:S(2)}) %all-to-all-start.8) | async-done | bytes 524320 | tf_op jit(solution)/shard_map/all_to_all | solution.py:106
  196.3 1.9 copy.126
  198.1 4.3 all-to-all-start.9
  202.5 1.3 fusion.50
  203.8 1.4 convolution_add_fusion.1
  205.2 7.0 %all-to-all-done.9 = bf16[4,8,16,512]{3,2,0,1:T(8,128)(2,1)S(1)} async-done(((bf16[4,8,16,512]{3,2,0,1:T(8,128)(2,1)}), bf16[4,8,16,512]{3,2,0,1:T(8,128)(2,1)S(1)}, u32[]{:S(2)}, u32[]{:S(2)}) %all-to-all-start.9) | async-done | bytes 524320 | tf_op jit(solution)/shard_map/all_to_all | solution.py:105
  212.5 3.8 scatter_fusion.1
  216.5 1.3 fusion.52
  217.9 1.3 convolution_bitcast_fusion
  219.5 101.3 %all-reduce.5.cloned.1.call-done = (f32[512,512]{0,1:T(8,128)}, f32[512,512]{0,1:T(8,128)}, f32[512,512]{0,1:T(8,128)}, f32[512,512]{0,1:T(8,128)}, f32[512,512]{0,1:T(8,128)}, /*index=5*/f32[512,512]{0,1:T(8,128)}) async-done(((f32[512,512]{0,1:T(8,128)}, f32[512,512]{0,1:T(8,128)}, f32[512,512]{0,1:T(8,128)}, f32[512,512]{0,1:T(8,128)}, f32[512,512]{0,1:T(8,128)}, /*index=5*/f32[512,512]{0,1:T(8,128)}), ...) | async-done | bytes 6291472 | tf_op jit(solution)/shard_map/psum | solution.py:9
  320.8 1.4 convolution_convert_fusion
  322.7 2.1 copy.134
  324.7 2.7 fusion.39
  327.8 34.8 %all_to_all.63 = bf16[4,8,16,512]{3,2,1,0:T(8,128)(2,1)S(1)} all-to-all(bf16[4,8,16,512]{3,2,1,0:T(8,128)(2,1)S(1)} %copy.136), channel_id=1, replica_groups=mesh['gx'=4,'gy'=8] {'gx'}, dimensions={0} | all-to-all | bytes 1048576 | tf_op jit(solution)/shard_map/all_to_all | solution.py:106
  363.4 3.7 all-to-all-start.11
  367.4 1.4 convolution_add_fusion
  368.8 8.0 %all-to-all-done.11 = bf16[4,8,16,512]{3,2,0,1:T(8,128)(2,1)S(1)} async-done(((bf16[4,8,16,512]{3,2,0,1:T(8,128)(2,1)}), bf16[4,8,16,512]{3,2,0,1:T(8,128)(2,1)S(1)}, u32[]{:S(2)}, u32[]{:S(2)}) %all-to-all-start.11) | async-done | bytes 524320 | tf_op jit(solution)/shard_map/all_to_all | solution.py:105
  377.1 3.8 scatter_fusion.2
  381.6 176.1 %all-reduce.7.cloned.1.call-done = (f32[512,512]{0,1:T(8,128)}, f32[512,512]{0,1:T(8,128)}, f32[512,512]{0,1:T(8,128)}, f32[512,512]{0,1:T(8,128)}, f32[512,512]{0,1:T(8,128)}, /*index=5*/f32[512,512]{0,1:T(8,128)}) async-done(((f32[512,512]{0,1:T(8,128)}, f32[512,512]{0,1:T(8,128)}, f32[512,512]{0,1:T(8,128)}, f32[512,512]{0,1:T(8,128)}, f32[512,512]{0,1:T(8,128)}, /*index=5*/f32[512,512]{0,1:T(8,128)}), ...) | async-done | bytes 6291472 | tf_op jit(solution)/shard_map/psum | solution.py:9
  557.8 2.0 fusion.7
  560.4 1.6 copy.140
  562.0 1.5 fusion.3
  563.7 1.6 copy.139
  (97 shorter events, 15.2 us)
Async XLA Ops:
  7.2 41.7 %copy-start = (bf16[2,4,128,128]{3,2,1,0:T(8,128)(2,1)S(1)}, bf16[2,4,128,128]{3,2,1,0:T(8,128)(2,1)}, u32[]{:S(2)}) copy-start(bf16[2,4,128,128]{3,2,1,0:T(8,128)(2,1)} %param.14) | copy-start | bytes 786436
  12.1 25.4 %copy-start.18 = (s32[2,4]{1,0:T(2,128)S(1)}, s32[2,4]{1,0:T(2,128)}, u32[]{:S(2)}) copy-start(s32[2,4]{1,0:T(2,128)} %param.15) | copy-start | bytes 100
  12.1 25.5 %copy-start.1 = (bf16[256,512]{1,0:T(8,128)(2,1)S(1)}, bf16[256,512]{1,0:T(8,128)(2,1)}, u32[]{:S(2)}) copy-start(bf16[256,512]{1,0:T(8,128)(2,1)} %param.10) | copy-start | bytes 786436
  12.1 25.5 %copy-start.2 = (bf16[3,512,512]{2,1,0:T(8,128)(2,1)S(1)}, bf16[3,512,512]{2,1,0:T(8,128)(2,1)}, u32[]{:S(2)}) copy-start(bf16[3,512,512]{2,1,0:T(8,128)(2,1)} %param.12) | copy-start | bytes 4718596
  33.8 13.4 %all-to-all-start.1 = ((bf16[4,8,16,512]{3,2,0,1:T(8,128)(2,1)}), bf16[4,8,16,512]{3,2,0,1:T(8,128)(2,1)S(1)}, u32[]{:S(2)}, u32[]{:S(2)}) async-start(bf16[4,8,16,512]{3,2,0,1:T(8,128)(2,1)} %copy.109), calls=%async_computation.1 | async-start | bytes 1048576 | tf_op jit(solution)/shard_map/all_to_all | solution.py:60
  48.9 1.6 copy-start.15
  50.5 2.3 copy-start.8
  70.7 14.0 %all-to-all-start.3 = ((bf16[4,8,16,512]{3,2,0,1:T(8,128)(2,1)}), bf16[4,8,16,512]{3,2,0,1:T(8,128)(2,1)S(1)}, u32[]{:S(2)}, u32[]{:S(2)}) async-start(bf16[4,8,16,512]{3,2,0,1:T(8,128)(2,1)} %copy.111), calls=%async_computation.3 | async-start | bytes 1048576 | tf_op jit(solution)/shard_map/all_to_all | solution.py:60
  86.4 1.6 copy-start.16
  88.0 2.3 copy-start.10
  108.2 14.0 %all-to-all-start.5 = ((bf16[4,8,16,512]{3,2,0,1:T(8,128)(2,1)}), bf16[4,8,16,512]{3,2,0,1:T(8,128)(2,1)S(1)}, u32[]{:S(2)}, u32[]{:S(2)}) async-start(bf16[4,8,16,512]{3,2,0,1:T(8,128)(2,1)} %copy.113), calls=%async_computation.5 | async-start | bytes 1048576 | tf_op jit(solution)/shard_map/all_to_all | solution.py:60
  122.9 1.0 copy-start.17
  123.0 1.1 copy-start.19
  123.3 2.3 copy-start.12
  125.6 31.2 %copy-start.3 = (bf16[256,512]{1,0:T(8,128)(2,1)}, bf16[256,512]{1,0:T(8,128)(2,1)S(1)}, u32[]{:S(2)}) copy-start(bf16[256,512]{1,0:T(8,128)(2,1)S(1)} %multiply_convert_fusion.8) | copy-start | bytes 786436
  133.5 16.7 %all-to-all-start.6 = ((bf16[4,8,16,512]{3,2,1,0:T(8,128)(2,1)}), bf16[4,8,16,512]{3,2,1,0:T(8,128)(2,1)}, u32[]{:S(2)}, u32[]{:S(2)}) async-start(bf16[4,8,16,512]{3,2,1,0:T(8,128)(2,1)} %copy.119), calls=%async_computation.6 | async-start | bytes 1048576 | tf_op jit(solution)/shard_map/all_to_all | solution.py:106
  152.1 14.1 %all-to-all-start.7 = ((bf16[4,8,16,512]{3,2,0,1:T(8,128)(2,1)}), bf16[4,8,16,512]{3,2,0,1:T(8,128)(2,1)}, u32[]{:S(2)}, u32[]{:S(2)}) async-start(bf16[4,8,16,512]{3,2,0,1:T(8,128)(2,1)} %copy.120), calls=%async_computation.7 | async-start | bytes 1048576 | tf_op jit(solution)/shard_map/all_to_all | solution.py:105
  167.5 4.0 copy-start.14
  179.5 16.7 %all-to-all-start.8 = ((bf16[4,8,16,512]{3,2,1,0:T(8,128)(2,1)}), bf16[4,8,16,512]{3,2,1,0:T(8,128)(2,1)}, u32[]{:S(2)}, u32[]{:S(2)}) async-start(bf16[4,8,16,512]{3,2,1,0:T(8,128)(2,1)} %copy.125), calls=%async_computation.8 | async-start | bytes 1048576 | tf_op jit(solution)/shard_map/all_to_all | solution.py:106
  183.7 2.4 copy-start.4
  186.1 1.7 copy-start.11
  198.1 14.0 %all-to-all-start.9 = ((bf16[4,8,16,512]{3,2,0,1:T(8,128)(2,1)}), bf16[4,8,16,512]{3,2,0,1:T(8,128)(2,1)S(1)}, u32[]{:S(2)}, u32[]{:S(2)}) async-start(bf16[4,8,16,512]{3,2,0,1:T(8,128)(2,1)} %copy.126), calls=%async_computation.9 | async-start | bytes 1048576 | tf_op jit(solution)/shard_map/all_to_all | solution.py:105
  202.5 118.3 %all-reduce.5.cloned.1.call-start = ((), (), s32[]{:S(2)}) async-start(), calls=%async_computation.12 | async-start | bytes 12582912 | tf_op jit(solution)/shard_map/psum | solution.py:9
  212.5 3.8 copy-start.13
  212.5 4.1 copy-start.9
  219.2 338.6 %all-reduce.7.cloned.1.call-start = ((), (), s32[]{:S(2)}) async-start(), calls=%async_computation.13 | async-start | bytes 12582912 | tf_op jit(solution)/shard_map/psum | solution.py:9
  363.4 13.4 %all-to-all-start.11 = ((bf16[4,8,16,512]{3,2,0,1:T(8,128)(2,1)}), bf16[4,8,16,512]{3,2,0,1:T(8,128)(2,1)S(1)}, u32[]{:S(2)}, u32[]{:S(2)}) async-start(bf16[4,8,16,512]{3,2,0,1:T(8,128)(2,1)} %copy.137), calls=%async_computation.11 | async-start | bytes 1048576 | tf_op jit(solution)/shard_map/all_to_all | solution.py:105
  557.8 2.0 copy-start.6
  557.8 2.2 copy-start.7
  560.4 1.6 copy-start.5
Sparse Core Ops, SparseCore 0:
  219.4 101.3 all-reduce.4
  323.6 234.1 all-reduce.6
